TPU v7x, 128 devices: a whole 4x4x4 slice. The times are simulated.
128 devices in a mesh: fsdp: 16 (over y, z), seq: 8 (over x, core).
Axes of the slice: x: 4, y: 4, z: 4, core: 2. Of those that a mesh axis runs over, the one named last changes fastest.
Arguments:
- frames: bfloat16 [16, 3072, 1536], P('fsdp', 'seq'), may hold values from -0.59765625 to 0.59765625
- lengths: int32 [16, 12], P('fsdp'), may hold values from 1 to 512, 3072 in all within a row
- w_qkv: bfloat16 [1536, 3072], P('fsdp'), may hold values from -4 to 4
- d_context: bfloat16 [16, 3072, 1024], P('fsdp', 'seq'), may hold values from -0.59765625 to 0.59765625
Outputs:
- context: bfloat16 [16, 3072, 1024], P('fsdp', 'seq')
- grad_input: bfloat16 [16, 3072, 1536], P('fsdp', 'seq')
- grad_weight: float32 [1536, 3072], P('fsdp', 'seq')
Inputs may be any that keep to these rules, and one draw needn't show every extreme that they name: The 12 lengths of a sequence sum to 3072, and the longest is exactly 512.
All inputs are finite; a program needn't handle non-finite values.
Results may differ from a plain program's by a relative error of at most 0.018.
Values may be sent and summed in bfloat16 or wider, within the bound.
A program may use at most 128 MiB of HBM per device.

v0:
```python
import jax
import jax.numpy as jnp
from jax import lax
from jax.sharding import PartitionSpec as P

HEADS = 16
HEAD_DIM = 64
MOST = 512


def segment_ids(lengths, frame_total):
    utter_ends = jnp.cumsum(lengths)
    positions = jnp.arange(frame_total, dtype=jnp.int32)
    return jnp.sum((positions[:, None] >= utter_ends[None, :]).astype(jnp.int32), axis=1)


def attend(query, keys, values, grad_out, segment):
    frame_total = query.shape[0]
    block_rows = 512
    key_span = min(block_rows + 2 * MOST, frame_total)
    block_count = frame_total // block_rows
    score_scale = HEAD_DIM ** (-0.5)

    def block_step(block_index, state_tuple):
        context, grad_query, grad_key, grad_value = state_tuple
        block_start = (block_index * block_rows).astype(jnp.int32)
        anchor = jnp.clip(block_start - MOST, 0, frame_total - key_span)
        query_block = lax.dynamic_slice_in_dim(query, block_start, block_rows, 0)
        grad_block = lax.dynamic_slice_in_dim(grad_out, block_start, block_rows, 0)
        segment_query = lax.dynamic_slice_in_dim(segment, block_start, block_rows, 0)
        key_window = lax.dynamic_slice_in_dim(keys, anchor, key_span, 0)
        value_window = lax.dynamic_slice_in_dim(values, anchor, key_span, 0)
        segment_key = lax.dynamic_slice_in_dim(segment, anchor, key_span, 0)
        scores = (
            jnp.einsum("qhd,khd->hqk", query_block, key_window, preferred_element_type=jnp.float32)
            * score_scale
        )
        same_utterance = segment_query[:, None] == segment_key[None, :]
        scores = jnp.where(same_utterance[None], scores, -jnp.inf)
        row_max = jnp.max(scores, axis=-1, keepdims=True)
        exponent = jnp.exp(scores - row_max)
        softmax_out = exponent / jnp.sum(exponent, axis=-1, keepdims=True)
        weights = softmax_out.astype(jnp.bfloat16)
        out_block = jnp.einsum(
            "hqk,khd->qhd", weights, value_window, preferred_element_type=jnp.float32
        ).astype(jnp.bfloat16)
        value_term = jnp.einsum(
            "hqk,qhd->khd", weights, grad_block, preferred_element_type=jnp.float32
        )
        dprobs = jnp.einsum(
            "qhd,khd->hqk", grad_block, value_window, preferred_element_type=jnp.float32
        )
        dscores = (
            softmax_out
            * (dprobs - jnp.sum(softmax_out * dprobs, axis=-1, keepdims=True))
            * score_scale
        )
        dscores = dscores.astype(jnp.bfloat16)
        query_term = jnp.einsum(
            "hqk,khd->qhd", dscores, key_window, preferred_element_type=jnp.float32
        ).astype(jnp.bfloat16)
        key_term = jnp.einsum(
            "hqk,qhd->khd", dscores, query_block, preferred_element_type=jnp.float32
        )
        context = lax.dynamic_update_slice_in_dim(context, out_block, block_start, 0)
        grad_query = lax.dynamic_update_slice_in_dim(grad_query, query_term, block_start, 0)
        grad_key = lax.dynamic_update_slice_in_dim(
            grad_key, lax.dynamic_slice_in_dim(grad_key, anchor, key_span, 0) + key_term, anchor, 0
        )
        grad_value = lax.dynamic_update_slice_in_dim(
            grad_value,
            lax.dynamic_slice_in_dim(grad_value, anchor, key_span, 0) + value_term,
            anchor,
            0,
        )
        return (context, grad_query, grad_key, grad_value)

    shape_one = query.shape
    initial = (
        jnp.zeros(shape_one, jnp.bfloat16),
        jnp.zeros(shape_one, jnp.bfloat16),
        jnp.zeros(shape_one, jnp.float32),
        jnp.zeros(shape_one, jnp.float32),
    )
    context, grad_query, grad_key, grad_value = lax.fori_loop(0, block_count, block_step, initial)
    return (context, grad_query, grad_key.astype(jnp.bfloat16), grad_value.astype(jnp.bfloat16))


def per_device(frames, lengths, w_qkv, d_context):
    values_in = frames[0].astype(jnp.float32)
    frame_count = values_in.shape[0]
    rank_count = lax.axis_size("seq")
    frame_total = frame_count * rank_count
    width = HEADS * HEAD_DIM
    per_rank = width // rank_count
    heads_here = per_rank // HEAD_DIM
    average = jnp.mean(values_in, axis=1, keepdims=True)
    centred = values_in - average
    variance = jnp.mean(centred * centred, axis=1, keepdims=True)
    inverse_scale = lax.rsqrt(variance + 1e-05)
    whitened = centred * inverse_scale
    normed = whitened.astype(jnp.bfloat16)
    weight_full = lax.all_gather(w_qkv, "fsdp", axis=0, tiled=True)
    projected = jnp.dot(normed, weight_full, preferred_element_type=jnp.float32)
    qkv_frames = projected.astype(jnp.bfloat16).reshape(frame_count, 3, rank_count, per_rank)
    cotangent = d_context[0].reshape(frame_count, 1, rank_count, per_rank)
    heads_qkv, heads_cotangent = (
        lax.all_to_all(qkv_frames, "seq", split_axis=2, concat_axis=0, tiled=True),
        lax.all_to_all(cotangent, "seq", split_axis=2, concat_axis=0, tiled=True),
    )
    query = heads_qkv[:, 0, 0].reshape(frame_total, heads_here, HEAD_DIM)
    keys = heads_qkv[:, 1, 0].reshape(frame_total, heads_here, HEAD_DIM)
    values = heads_qkv[:, 2, 0].reshape(frame_total, heads_here, HEAD_DIM)
    grad_out = heads_cotangent[:, 0, 0].reshape(frame_total, heads_here, HEAD_DIM)
    segment = segment_ids(lengths[0], frame_total)
    context, grad_query, grad_key, grad_value = attend(query, keys, values, grad_out, segment)
    context_heads = context.reshape(frame_total, 1, 1, per_rank)
    grad_heads = jnp.stack([grad_query, grad_key, grad_value], axis=1).reshape(
        frame_total, 3, 1, per_rank
    )
    context_back, grad_back = (
        lax.all_to_all(context_heads, "seq", split_axis=0, concat_axis=2, tiled=True),
        lax.all_to_all(grad_heads, "seq", split_axis=0, concat_axis=2, tiled=True),
    )
    context_out = context_back.reshape(1, frame_count, width)
    grad_qkv = grad_back.reshape(frame_count, 3 * width)
    grad_normed = lax.dot_general(
        grad_qkv, weight_full, (((1,), (1,)), ((), ())), preferred_element_type=jnp.float32
    )
    grad_input = inverse_scale * (
        grad_normed
        - jnp.mean(grad_normed, axis=1, keepdims=True)
        - whitened * jnp.mean(grad_normed * whitened, axis=1, keepdims=True)
    )
    grad_input = grad_input.astype(jnp.bfloat16)[None]
    owned_rows = lax.psum_scatter(
        lax.dot_general(
            normed, grad_qkv, (((0,), (0,)), ((), ())), preferred_element_type=jnp.float32
        ).astype(jnp.bfloat16),
        "fsdp",
        scatter_dimension=0,
        tiled=True,
    )
    grad_weight = lax.psum_scatter(owned_rows, "seq", scatter_dimension=1, tiled=True).astype(
        jnp.float32
    )
    return (context_out, grad_input, grad_weight)


def solution(mesh):
    return jax.shard_map(
        per_device,
        mesh=mesh,
        in_specs=(P("fsdp", "seq", None), P("fsdp", None), P("fsdp", None), P("fsdp", "seq", None)),
        out_specs=(P("fsdp", "seq", None), P("fsdp", "seq", None), P("fsdp", "seq")),
        check_vma=False,
    )
```

profile of v0, /device:TPU:0, one launch (start us, length us, event | category | flops | bytes accessed | tf_op | source)
XLA Modules:
  0.0 692.2 jit_solution(15582703184175243166)
XLA Ops:
  15.3 73.1 %all-gather.2.cloned.1.call-done = bf16[1536,3072]{1,0:T(8,128)(2,1)} async-done(((bf16[96,3072]{1,0:T(8,128)(2,1)}), bf16[1536,3072]{1,0:T(8,128)(2,1)}) %all-gather.2.cloned.1.call-update) | async-done | bytes 9437200 | tf_op jit(solution)/shard_map/all_gather | solution.py:103
  88.4 7.9 %fusion.104 = bf16[48,8,24,128]{3,1,2,0:T(8,128)(2,1)S(1)} fusion(bf16[1536,3072]{1,0:T(8,128)(2,1)} %all-gather.2.cloned.1.call-done, bf16[1,384,1536]{2,1,0:T(8,128)(2,1)S(1)} %copy-done, f32[384]{0:T(512)S(1)} %add_rsqrt_fusion, f32[384]{0:T(512)S(1)} %broadcast_multiply_fusion.2), kind=kOutput, calls=%fused_computation.73 | convolution fusion | flops 3627417600 | bytes 12979200 | tf_op jit(solution)/shard_map/dot_general | solution.py:104
  107.2 26.0 %all-to-all-done = bf16[384,3,8,128]{3,0,1,2:T(8,128)(2,1)S(1)} async-done(((bf16[384,3,8,128]{3,0,1,2:T(8,128)(2,1)}), bf16[384,3,8,128]{3,0,1,2:T(8,128)(2,1)S(1)}, u32[]{:S(2)}, u32[]{:S(2)}) %all-to-all-start) | async-done | bytes 2359328 | tf_op jit(solution)/shard_map/all_to_all | solution.py:108
  139.9 362.4 %while.21 = (s32[]{:T(128)}, bf16[3072,2,64]{0,2,1:T(8,128)(2,1)S(1)}, bf16[3072,2,64]{0,2,1:T(8,128)(2,1)}, f32[3072,2,64]{0,2,1:T(8,128)}, f32[3072,2,64]{0,2,...) while((s32[]{:T(128)}, ...), condition=%wide.region_8.9_spmd, body=%wide.region_4.8_spmd.sunk | while | flops 1655975424 | bytes 78963000 | solution.py:85
  155.5 14.9 %fusion.165 = bf16[3072,2,64]{0,2,1:T(8,128)(2,1)} fusion(bf16[3072,2,64]{0,2,1:T(8,128)(2,1)} %get-tuple-element.393, s32[]{:T(128)S(6)} %select_n.55, f32[2,512,1536]{2,1,0:T(8,128)} %fusion.164, bf16[3072,2,64]{0,2,1:T(8,128)(2,1)S(1)} %copy-done.5, s32[]{:T(128)S(6)} %min.12, f32[2,512,1536]{2,1,0:T(8,128)} %get-tuple-element.374, ...), kind=kOutput, calls=%fused_computation.27.clone.1 | convolution fusion | flops 212404736 | bytes 25698312 | tf_op jit(solution)/shard_map/while/body/eval_jaxpr/hqk,khd->qhd/dot_general | solution.py:59
  170.3 14.9 %fusion.166 = f32[1536,2,64]{0,2,1:T(8,128)S(1)} fusion(f32[2,512,1536]{2,1,0:T(8,128)} %fusion.164, f32[3072,2,64]{0,2,1:T(8,128)} %get-tuple-element.394, s32[]{:T(128)S(6)} %min.12, bf16[3072,2,64]{0,2,1:T(8,128)(2,1)} %get-tuple-element.414, s32[]{:T(128)S(6)} %select_n.55, f32[2,512,1536]{2,1,0:T(8,128)} %get-tuple-element.374, ...), kind=kOutput, calls=%fused_computation.17.clone.1 | convolution fusion | flops 212535808 | bytes 26877960 | tf_op jit(solution)/shard_map/while/body/eval_jaxpr/hqk,qhd->khd/dot_general | solution.py:62
  201.5 6.2 fusion.162
  216.3 14.9 %fusion.165 = bf16[3072,2,64]{0,2,1:T(8,128)(2,1)} fusion(bf16[3072,2,64]{0,2,1:T(8,128)(2,1)} %get-tuple-element.393, s32[]{:T(128)S(6)} %select_n.55, f32[2,512,1536]{2,1,0:T(8,128)} %fusion.164, bf16[3072,2,64]{0,2,1:T(8,128)(2,1)S(1)} %copy-done.5, s32[]{:T(128)S(6)} %min.12, f32[2,512,1536]{2,1,0:T(8,128)} %get-tuple-element.374, ...), kind=kOutput, calls=%fused_computation.27.clone.1 | convolution fusion | flops 212404736 | bytes 25698312 | tf_op jit(solution)/shard_map/while/body/eval_jaxpr/hqk,khd->qhd/dot_general | solution.py:59
  231.2 15.0 %fusion.166 = f32[1536,2,64]{0,2,1:T(8,128)S(1)} fusion(f32[2,512,1536]{2,1,0:T(8,128)} %fusion.164, f32[3072,2,64]{0,2,1:T(8,128)} %get-tuple-element.394, s32[]{:T(128)S(6)} %min.12, bf16[3072,2,64]{0,2,1:T(8,128)(2,1)} %get-tuple-element.414, s32[]{:T(128)S(6)} %select_n.55, f32[2,512,1536]{2,1,0:T(8,128)} %get-tuple-element.374, ...), kind=kOutput, calls=%fused_computation.17.clone.1 | convolution fusion | flops 212535808 | bytes 26877960 | tf_op jit(solution)/shard_map/while/body/eval_jaxpr/hqk,qhd->khd/dot_general | solution.py:62
  277.3 14.9 %fusion.165 = bf16[3072,2,64]{0,2,1:T(8,128)(2,1)} fusion(bf16[3072,2,64]{0,2,1:T(8,128)(2,1)} %get-tuple-element.393, s32[]{:T(128)S(6)} %select_n.55, f32[2,512,1536]{2,1,0:T(8,128)} %fusion.164, bf16[3072,2,64]{0,2,1:T(8,128)(2,1)S(1)} %copy-done.5, s32[]{:T(128)S(6)} %min.12, f32[2,512,1536]{2,1,0:T(8,128)} %get-tuple-element.374, ...), kind=kOutput, calls=%fused_computation.27.clone.1 | convolution fusion | flops 212404736 | bytes 25698312 | tf_op jit(solution)/shard_map/while/body/eval_jaxpr/hqk,khd->qhd/dot_general | solution.py:59
  292.2 14.9 %fusion.166 = f32[1536,2,64]{0,2,1:T(8,128)S(1)} fusion(f32[2,512,1536]{2,1,0:T(8,128)} %fusion.164, f32[3072,2,64]{0,2,1:T(8,128)} %get-tuple-element.394, s32[]{:T(128)S(6)} %min.12, bf16[3072,2,64]{0,2,1:T(8,128)(2,1)} %get-tuple-element.414, s32[]{:T(128)S(6)} %select_n.55, f32[2,512,1536]{2,1,0:T(8,128)} %get-tuple-element.374, ...), kind=kOutput, calls=%fused_computation.17.clone.1 | convolution fusion | flops 212535808 | bytes 26877960 | tf_op jit(solution)/shard_map/while/body/eval_jaxpr/hqk,qhd->khd/dot_general | solution.py:62
  323.2 6.2 fusion.162
  338.0 14.9 %fusion.165 = bf16[3072,2,64]{0,2,1:T(8,128)(2,1)} fusion(bf16[3072,2,64]{0,2,1:T(8,128)(2,1)} %get-tuple-element.393, s32[]{:T(128)S(6)} %select_n.55, f32[2,512,1536]{2,1,0:T(8,128)} %fusion.164, bf16[3072,2,64]{0,2,1:T(8,128)(2,1)S(1)} %copy-done.5, s32[]{:T(128)S(6)} %min.12, f32[2,512,1536]{2,1,0:T(8,128)} %get-tuple-element.374, ...), kind=kOutput, calls=%fused_computation.27.clone.1 | convolution fusion | flops 212404736 | bytes 25698312 | tf_op jit(solution)/shard_map/while/body/eval_jaxpr/hqk,khd->qhd/dot_general | solution.py:59
  352.9 15.0 %fusion.166 = f32[1536,2,64]{0,2,1:T(8,128)S(1)} fusion(f32[2,512,1536]{2,1,0:T(8,128)} %fusion.164, f32[3072,2,64]{0,2,1:T(8,128)} %get-tuple-element.394, s32[]{:T(128)S(6)} %min.12, bf16[3072,2,64]{0,2,1:T(8,128)(2,1)} %get-tuple-element.414, s32[]{:T(128)S(6)} %select_n.55, f32[2,512,1536]{2,1,0:T(8,128)} %get-tuple-element.374, ...), kind=kOutput, calls=%fused_computation.17.clone.1 | convolution fusion | flops 212535808 | bytes 26877960 | tf_op jit(solution)/shard_map/while/body/eval_jaxpr/hqk,qhd->khd/dot_general | solution.py:62
  398.6 14.9 %fusion.165 = bf16[3072,2,64]{0,2,1:T(8,128)(2,1)} fusion(bf16[3072,2,64]{0,2,1:T(8,128)(2,1)} %get-tuple-element.393, s32[]{:T(128)S(6)} %select_n.55, f32[2,512,1536]{2,1,0:T(8,128)} %fusion.164, bf16[3072,2,64]{0,2,1:T(8,128)(2,1)S(1)} %copy-done.5, s32[]{:T(128)S(6)} %min.12, f32[2,512,1536]{2,1,0:T(8,128)} %get-tuple-element.374, ...), kind=kOutput, calls=%fused_computation.27.clone.1 | convolution fusion | flops 212404736 | bytes 25698312 | tf_op jit(solution)/shard_map/while/body/eval_jaxpr/hqk,khd->qhd/dot_general | solution.py:59
  413.5 14.9 %fusion.166 = f32[1536,2,64]{0,2,1:T(8,128)S(1)} fusion(f32[2,512,1536]{2,1,0:T(8,128)} %fusion.164, f32[3072,2,64]{0,2,1:T(8,128)} %get-tuple-element.394, s32[]{:T(128)S(6)} %min.12, bf16[3072,2,64]{0,2,1:T(8,128)(2,1)} %get-tuple-element.414, s32[]{:T(128)S(6)} %select_n.55, f32[2,512,1536]{2,1,0:T(8,128)} %get-tuple-element.374, ...), kind=kOutput, calls=%fused_computation.17.clone.1 | convolution fusion | flops 212535808 | bytes 26877960 | tf_op jit(solution)/shard_map/while/body/eval_jaxpr/hqk,qhd->khd/dot_general | solution.py:62
  458.2 14.9 %fusion.165 = bf16[3072,2,64]{0,2,1:T(8,128)(2,1)} fusion(bf16[3072,2,64]{0,2,1:T(8,128)(2,1)} %get-tuple-element.393, s32[]{:T(128)S(6)} %select_n.55, f32[2,512,1536]{2,1,0:T(8,128)} %fusion.164, bf16[3072,2,64]{0,2,1:T(8,128)(2,1)S(1)} %copy-done.5, s32[]{:T(128)S(6)} %min.12, f32[2,512,1536]{2,1,0:T(8,128)} %get-tuple-element.374, ...), kind=kOutput, calls=%fused_computation.27.clone.1 | convolution fusion | flops 212404736 | bytes 25698312 | tf_op jit(solution)/shard_map/while/body/eval_jaxpr/hqk,khd->qhd/dot_general | solution.py:59
  473.1 15.0 %fusion.166 = f32[1536,2,64]{0,2,1:T(8,128)S(1)} fusion(f32[2,512,1536]{2,1,0:T(8,128)} %fusion.164, f32[3072,2,64]{0,2,1:T(8,128)} %get-tuple-element.394, s32[]{:T(128)S(6)} %min.12, bf16[3072,2,64]{0,2,1:T(8,128)(2,1)} %get-tuple-element.414, s32[]{:T(128)S(6)} %select_n.55, f32[2,512,1536]{2,1,0:T(8,128)} %get-tuple-element.374, ...), kind=kOutput, calls=%fused_computation.17.clone.1 | convolution fusion | flops 212535808 | bytes 26877960 | tf_op jit(solution)/shard_map/while/body/eval_jaxpr/hqk,qhd->khd/dot_general | solution.py:62
  511.8 40.9 %all_to_all.63 = bf16[3072,3,1,128]{3,1,2,0:T(4,128)(2,1)S(1)} all-to-all(bf16[3072,3,1,128]{3,1,2,0:T(4,128)(2,1)S(1)} %copy.83), channel_id=1, replica_groups=mesh['fsdp'=16,'seq'=8] {'seq'}, dimensions={0} | all-to-all | bytes 4718592 | tf_op jit(solution)/shard_map/all_to_all | solution.py:123
  555.5 9.5 %convolution_convert_fusion = bf16[1536,3072]{1,0:T(8,128)(2,1)} fusion(bf16[384,3072]{0,1:T(8,128)(2,1)} %bitcast.107, bf16[1,384,1536]{2,1,0:T(8,128)(2,1)S(1)} %copy-done.1, f32[384]{0:T(512)S(1)} %copy-done.9, f32[384]{0:T(512)S(1)} %copy-done.7), kind=kOutput, calls=%fused_computation.54 | convolution fusion | flops 3630956544 | bytes 12979200 | tf_op jit(solution)/shard_map/dot_general | solution.py:137
  568.0 15.6 %all_to_all.64 = bf16[8,2,24576]{2,1,0:T(2,128)(2,1)S(1)} all-to-all(bf16[8,2,24576]{2,1,0:T(2,128)(2,1)S(1)} %reshape.126), channel_id=1, replica_groups=mesh['fsdp'=16,'seq'=8] {'seq'}, dimensions={0} | all-to-all | bytes 1572864 | tf_op jit(solution)/shard_map/all_to_all | solution.py:122
  586.0 64.8 %reduce-scatter.5.cloned.1.call-done = bf16[96,3072]{1,0:T(8,128)(2,1)} async-done(((bf16[1536,3072]{1,0:T(8,128)(2,1)}), bf16[96,3072]{1,0:T(8,128)(2,1)}) %reduce-scatter.5.cloned.1.call-update) | async-done | bytes 589840 | tf_op jit(solution)/shard_map/reduce_scatter | solution.py:136
  653.0 7.7 %fusion.113 = (f32[384]{0:T(512)S(1)}, f32[384]{0:T(512)S(1)}, f32[384,1536]{1,0:T(8,128)S(1)}) fusion(f32[384]{0:T(512)S(1)} %copy-done.9, f32[384]{0:T(512)S(1)} %copy-done.7, bf16[1,384,1536]{2,1,0:T(8,128)(2,1)S(1)} %copy-done.1, bf16[384,3072]{0,1:T(8,128)(2,1)} %bitcast.108, bf16[1536,3072]{1,0:T(8,128)(2,1)} %all-gather.2.cloned.1.call-done), kind=kOutput, calls=%fused_computation.86 | convolution fusion | flops 3627416576 | bytes 15341568 | tf_op jit(solution)/shard_map/dot_general | solution.py:127
  662.4 21.6 %reduce-scatter.7.cloned.1.call-done = bf16[384,96]{1,0:T(8,128)(2,1)} async-done(((bf16[3072,96]{1,0:T(8,128)(2,1)}), bf16[384,96]{1,0:T(8,128)(2,1)}) %reduce-scatter.7.cloned.1.call-update) | async-done | bytes 73744
  (132 shorter events, 219.8 us)
Async XLA Ops:
  7.2 7.4 %copy-start = (bf16[1,384,1536]{2,1,0:T(8,128)(2,1)S(1)}, bf16[1,384,1536]{2,1,0:T(8,128)(2,1)}, u32[]{:S(2)}) copy-start(bf16[1,384,1536]{2,1,0:T(8,128)(2,1)} %param.6) | copy-start | bytes 3538948
  7.2 81.2 %all-gather.2.cloned.1.call-start = ((), (), s32[]{:S(2)}) async-start(), calls=%async_computation.6 | async-start | bytes 10027008 | tf_op jit(solution)/shard_map/all_gather | solution.py:103
  10.2 88.6 %all-to-all-start.1 = ((bf16[384,1,8,128]{0,3,1,2:T(8,128)(2,1)}), bf16[384,1,8,128]{0,3,1,2:T(8,128)(2,1)S(1)}, u32[]{:S(2)}, u32[]{:S(2)}) async-start(bf16[384,1,8,128]{0,3,1,2:T(8,128)(2,1)} %bitcast.15), calls=%async_computation.1 | async-start | bytes 1572864 | tf_op jit(solution)/shard_map/all_to_all | solution.py:109
  14.9 81.4 %copy-start.6 = (f32[384]{0:T(512)}, f32[384]{0:T(512)S(1)}, u32[]{:S(2)}) copy-start(f32[384]{0:T(512)S(1)} %broadcast_multiply_fusion.2) | copy-start | bytes 4612
  15.3 81.0 %copy-start.8 = (f32[384]{0:T(512)}, f32[384]{0:T(512)S(1)}, u32[]{:S(2)}) copy-start(f32[384]{0:T(512)S(1)} %add_rsqrt_fusion) | copy-start | bytes 4612
  98.8 4.4 copy-start.10
  98.8 34.4 %all-to-all-start = ((bf16[384,3,8,128]{3,0,1,2:T(8,128)(2,1)}), bf16[384,3,8,128]{3,0,1,2:T(8,128)(2,1)S(1)}, u32[]{:S(2)}, u32[]{:S(2)}) async-start(bf16[384,3,8,128]{3,0,1,2:T(8,128)(2,1)} %copy.74), calls=%async_computation | async-start | bytes 4718592 | tf_op jit(solution)/shard_map/all_to_all | solution.py:108
  103.2 547.6 %reduce-scatter.5.cloned.1.call-start = ((), (), s32[]{:S(2)}) async-start(), calls=%async_computation.7 | async-start | bytes 10027008 | tf_op jit(solution)/shard_map/reduce_scatter | solution.py:136
  140.6 6.2 copy-start.5
  201.5 6.2 copy-start.5
  262.4 6.2 copy-start.5
  323.2 6.2 copy-start.5
  383.8 6.2 copy-start.5
  443.4 6.2 copy-start.5
  502.3 2.3 copy-start.3
  502.3 2.2 copy-start.2
  553.0 2.5 copy-start.1
  553.0 2.5 copy-start.7
  553.0 2.5 copy-start.9
  565.1 1.1 copy-start.4
  565.1 118.9 %reduce-scatter.7.cloned.1.call-start = ((), (), s32[]{:S(2)}) async-start(), calls=%async_computation.8 | async-start | bytes 884736
Sparse Core Ops, SparseCore 0:
  10.2 78.1 all-gather.1
  565.2 85.5 reduce-scatter.4
  653.2 30.7 reduce-scatter.6
where the time goes:
time: 695 us; the launch traced here: 692 us
  matrix products  320 us (46%)
  waiting for transfers between devices  186 us (27%)
  local copies, waits for them, and re-layouts  93.8 us (13%)
  blocking collectives  56.5 us (8%)
  between operations  14 us (2%)
  other arithmetic  12.3 us (2%)
  starting transfers between devices  8.91 us (1%)
    dot_general x6, matrix products, block_step(): jnp.einsum('hqk,qhd->khd', dscores, query_block, preferred_element_type=j...  89.7 us
    dot_general x6, matrix products, block_step(): jnp.einsum('hqk,khd->qhd', dscores, key_window, preferred_element_type=jn...  89.2 us
    all_gather x1, waiting for transfers between devices, per_device(): weight_full = lax.all_gather(w_qkv, 'fsdp', axis=0, tiled=True)  73.1 us
    reduce_scatter x1, waiting for transfers between devices, per_device(): lax.psum_scatter(lax.dot_general(normed, grad_qkv, (((0,), (0,)), ((), ()...  64.8 us
    all_to_all x1, blocking collectives, per_device(): lax.all_to_all(grad_heads, 'seq', split_axis=0, concat_axis=2, tiled=True)  40.9 us
    sub x6, matrix products, block_step(): exponent = jnp.exp(scores - row_max)  37.2 us
    dynamic_update_slice x6, local copies, waits for them, and re-layouts, block_step(): lax.dynamic_update_slice_in_dim(grad_value, lax.dynamic_slice_in_dim(grad...  31.5 us
    dynamic_update_slice x6, local copies, waits for them, and re-layouts, block_step(): lax.dynamic_update_slice_in_dim(grad_key, lax.dynamic_slice_in_dim(grad_k...  31.5 us
  transfers between devices with their start and end apart: 5, of which 4 were waited for; matrix products, arithmetic and copies ran while one was open for 5% of the time, Pallas kernels for 0%

commit v1 on v0

--- a/solution.py
+++ b/solution.py
@@ -100,7 +100,9 @@
     inverse_scale = lax.rsqrt(variance + 1e-05)
     whitened = centred * inverse_scale
     normed = whitened.astype(jnp.bfloat16)
-    weight_full = lax.all_gather(w_qkv, "fsdp", axis=0, tiled=True)
+    weight_full = jnp.concatenate(
+        lax.all_to_all(jnp.stack([w_qkv] * lax.axis_size("fsdp")), "fsdp", 0, 0), axis=0
+    )
     projected = jnp.dot(normed, weight_full, preferred_element_type=jnp.float32)
     qkv_frames = projected.astype(jnp.bfloat16).reshape(frame_count, 3, rank_count, per_rank)
     cotangent = d_context[0].reshape(frame_count, 1, rank_count, per_rank)

time: 695 us -> 807 us (1.16)
  waiting for transfers between devices: 186 us -> 285 us
    all_to_all x0 -> x1, waiting for transfers between devices: none -> 163 us  [per_device(): lax.all_to_all(jnp.stack([w_qkv] * lax.axis_size('fsdp')), 'fsdp', 0, 0)]
    all_gather x1 -> x0, waiting for transfers between devices: 73.1 us -> none  [per_device(): weight_full = lax.all_gather(w_qkv, 'fsdp', axis=0, tiled=True)]
    all_to_all x0 -> x1, starting transfers between devices: none -> 8.34 us  [per_device(): lax.all_to_all(jnp.stack([w_qkv] * lax.axis_size('fsdp')), 'fsdp', 0, 0)]
    unnamed x4 -> x3, waiting for transfers between devices: 22.3 us -> 21.7 us
  transfers between devices with their start and end apart: 5 -> 5, of which waited for: 4 -> 5; matrix products, arithmetic and copies ran while one was open for 5% -> 4% of each run, Pallas kernels for 0% -> 0%
where the time goes in v1:
time: 807 us; the launch traced here: 803 us
  matrix products  320 us (40%)
  waiting for transfers between devices  285 us (35%)
  local copies, waits for them, and re-layouts  98.6 us (12%)
  blocking collectives  56.5 us (7%)
  starting transfers between devices  16.3 us (2%)
  between operations  14.3 us (2%)
  other arithmetic  12.3 us (2%)
    all_to_all x1, waiting for transfers between devices, per_device(): lax.all_to_all(jnp.stack([w_qkv] * lax.axis_size('fsdp')), 'fsdp', 0, 0)  163 us
    dot_general x6, matrix products, block_step(): jnp.einsum('hqk,qhd->khd', dscores, query_block, preferred_element_type=j...  89.7 us
    dot_general x6, matrix products, block_step(): jnp.einsum('hqk,khd->qhd', dscores, key_window, preferred_element_type=jn...  89.2 us
    reduce_scatter x1, waiting for transfers between devices, per_device(): lax.psum_scatter(lax.dot_general(normed, grad_qkv, (((0,), (0,)), ((), ()...  71.7 us
    all_to_all x1, blocking collectives, per_device(): lax.all_to_all(grad_heads, 'seq', split_axis=0, concat_axis=2, tiled=True)  40.9 us
    sub x6, matrix products, block_step(): exponent = jnp.exp(scores - row_max)  37.2 us
    dynamic_update_slice x6, local copies, waits for them, and re-layouts, block_step(): lax.dynamic_update_slice_in_dim(grad_value, lax.dynamic_slice_in_dim(grad...  31.5 us
    dynamic_update_slice x6, local copies, waits for them, and re-layouts, block_step(): lax.dynamic_update_slice_in_dim(grad_key, lax.dynamic_slice_in_dim(grad_k...  31.5 us
  transfers between devices with their start and end apart: 5, of which 5 were waited for; matrix products, arithmetic and copies ran while one was open for 4% of the time, Pallas kernels for 0%

profile of v1, /device:TPU:0, one launch (start us, length us, event | category | flops | bytes accessed | tf_op | source)
XLA Modules:
  0.0 803.4 jit_solution(5498121945023722135)
XLA Ops:
  13.1 8.3 %all-to-all-start = ((bf16[16,96,3072]{2,1,0:T(8,128)(2,1)}), bf16[16,96,3072]{2,1,0:T(8,128)(2,1)}, u32[]{:S(2)}, u32[]{:S(2)}) async-start(bf16[16,96,3072]{2,1,0:T(8,128)(2,1)} %stack.10), calls=%async_computation | async-start | bytes 18874368 | tf_op jit(solution)/shard_map/all_to_all | solution.py:104
  23.3 162.8 %all-to-all-done = bf16[16,96,3072]{2,1,0:T(8,128)(2,1)} async-done(((bf16[16,96,3072]{2,1,0:T(8,128)(2,1)}), bf16[16,96,3072]{2,1,0:T(8,128)(2,1)}, u32[]{:S(2)}, u32[]{:S(2)}) %all-to-all-start) | async-done | bytes 9437216 | tf_op jit(solution)/shard_map/all_to_all | solution.py:104
  190.4 7.9 fusion.103
  211.1 26.0 %all-to-all-done.1 = bf16[384,3,8,128]{3,0,1,2:T(8,128)(2,1)S(1)} async-done(((bf16[384,3,8,128]{3,0,1,2:T(8,128)(2,1)}), bf16[384,3,8,128]{3,0,1,2:T(8,128)(2,1)S(1)}, u32[]{:S(2)}, u32[]{:S(2)}) %all-to-all-start.1) | async-done | bytes 2359328 | tf_op jit(solution)/shard_map/all_to_all | solution.py:110
  243.8 362.4 %while.21 = (s32[]{:T(128)}, bf16[3072,2,64]{0,2,1:T(8,128)(2,1)S(1)}, bf16[3072,2,64]{0,2,1:T(8,128)(2,1)}, f32[3072,2,64]{0,2,1:T(8,128)}, f32[3072,2,64]{0,2,...) while((s32[]{:T(128)}, ...), condition=%wide.region_8.9_spmd, body=%wide.region_4.8_spmd.sunk | while | flops 1655975424 | bytes 78963000 | solution.py:85
  244.5 6.2 fusion.157
  259.3 14.9 %fusion.160 = bf16[3072,2,64]{0,2,1:T(8,128)(2,1)} fusion(bf16[3072,2,64]{0,2,1:T(8,128)(2,1)} %get-tuple-element.393, s32[]{:T(128)S(6)} %select_n.55, f32[2,512,1536]{2,1,0:T(8,128)} %fusion.159, bf16[3072,2,64]{0,2,1:T(8,128)(2,1)S(1)} %copy-done.6, s32[]{:T(128)S(6)} %min.12, f32[2,512,1536]{2,1,0:T(8,128)} %get-tuple-element.374, ...), kind=kOutput, calls=%fused_computation.27.clone.1 | convolution fusion | flops 212404736 | bytes 25698312 | tf_op jit(solution)/shard_map/while/body/eval_jaxpr/hqk,khd->qhd/dot_general | solution.py:59
  274.2 14.9 %fusion.161 = f32[1536,2,64]{0,2,1:T(8,128)S(1)} fusion(f32[2,512,1536]{2,1,0:T(8,128)} %fusion.159, f32[3072,2,64]{0,2,1:T(8,128)} %get-tuple-element.394, s32[]{:T(128)S(6)} %min.12, bf16[3072,2,64]{0,2,1:T(8,128)(2,1)} %get-tuple-element.414, s32[]{:T(128)S(6)} %select_n.55, f32[2,512,1536]{2,1,0:T(8,128)} %get-tuple-element.374, ...), kind=kOutput, calls=%fused_computation.17.clone.1 | convolution fusion | flops 212535808 | bytes 26877960 | tf_op jit(solution)/shard_map/while/body/eval_jaxpr/hqk,qhd->khd/dot_general | solution.py:62
  320.2 14.9 %fusion.160 = bf16[3072,2,64]{0,2,1:T(8,128)(2,1)} fusion(bf16[3072,2,64]{0,2,1:T(8,128)(2,1)} %get-tuple-element.393, s32[]{:T(128)S(6)} %select_n.55, f32[2,512,1536]{2,1,0:T(8,128)} %fusion.159, bf16[3072,2,64]{0,2,1:T(8,128)(2,1)S(1)} %copy-done.6, s32[]{:T(128)S(6)} %min.12, f32[2,512,1536]{2,1,0:T(8,128)} %get-tuple-element.374, ...), kind=kOutput, calls=%fused_computation.27.clone.1 | convolution fusion | flops 212404736 | bytes 25698312 | tf_op jit(solution)/shard_map/while/body/eval_jaxpr/hqk,khd->qhd/dot_general | solution.py:59
  335.1 15.0 %fusion.161 = f32[1536,2,64]{0,2,1:T(8,128)S(1)} fusion(f32[2,512,1536]{2,1,0:T(8,128)} %fusion.159, f32[3072,2,64]{0,2,1:T(8,128)} %get-tuple-element.394, s32[]{:T(128)S(6)} %min.12, bf16[3072,2,64]{0,2,1:T(8,128)(2,1)} %get-tuple-element.414, s32[]{:T(128)S(6)} %select_n.55, f32[2,512,1536]{2,1,0:T(8,128)} %get-tuple-element.374, ...), kind=kOutput, calls=%fused_computation.17.clone.1 | convolution fusion | flops 212535808 | bytes 26877960 | tf_op jit(solution)/shard_map/while/body/eval_jaxpr/hqk,qhd->khd/dot_general | solution.py:62
  381.2 14.9 %fusion.160 = bf16[3072,2,64]{0,2,1:T(8,128)(2,1)} fusion(bf16[3072,2,64]{0,2,1:T(8,128)(2,1)} %get-tuple-element.393, s32[]{:T(128)S(6)} %select_n.55, f32[2,512,1536]{2,1,0:T(8,128)} %fusion.159, bf16[3072,2,64]{0,2,1:T(8,128)(2,1)S(1)} %copy-done.6, s32[]{:T(128)S(6)} %min.12, f32[2,512,1536]{2,1,0:T(8,128)} %get-tuple-element.374, ...), kind=kOutput, calls=%fused_computation.27.clone.1 | convolution fusion | flops 212404736 | bytes 25698312 | tf_op jit(solution)/shard_map/while/body/eval_jaxpr/hqk,khd->qhd/dot_general | solution.py:59
  396.0 14.9 %fusion.161 = f32[1536,2,64]{0,2,1:T(8,128)S(1)} fusion(f32[2,512,1536]{2,1,0:T(8,128)} %fusion.159, f32[3072,2,64]{0,2,1:T(8,128)} %get-tuple-element.394, s32[]{:T(128)S(6)} %min.12, bf16[3072,2,64]{0,2,1:T(8,128)(2,1)} %get-tuple-element.414, s32[]{:T(128)S(6)} %select_n.55, f32[2,512,1536]{2,1,0:T(8,128)} %get-tuple-element.374, ...), kind=kOutput, calls=%fused_computation.17.clone.1 | convolution fusion | flops 212535808 | bytes 26877960 | tf_op jit(solution)/shard_map/while/body/eval_jaxpr/hqk,qhd->khd/dot_general | solution.py:62
  441.9 14.9 %fusion.160 = bf16[3072,2,64]{0,2,1:T(8,128)(2,1)} fusion(bf16[3072,2,64]{0,2,1:T(8,128)(2,1)} %get-tuple-element.393, s32[]{:T(128)S(6)} %select_n.55, f32[2,512,1536]{2,1,0:T(8,128)} %fusion.159, bf16[3072,2,64]{0,2,1:T(8,128)(2,1)S(1)} %copy-done.6, s32[]{:T(128)S(6)} %min.12, f32[2,512,1536]{2,1,0:T(8,128)} %get-tuple-element.374, ...), kind=kOutput, calls=%fused_computation.27.clone.1 | convolution fusion | flops 212404736 | bytes 25698312 | tf_op jit(solution)/shard_map/while/body/eval_jaxpr/hqk,khd->qhd/dot_general | solution.py:59
  456.8 15.0 %fusion.161 = f32[1536,2,64]{0,2,1:T(8,128)S(1)} fusion(f32[2,512,1536]{2,1,0:T(8,128)} %fusion.159, f32[3072,2,64]{0,2,1:T(8,128)} %get-tuple-element.394, s32[]{:T(128)S(6)} %min.12, bf16[3072,2,64]{0,2,1:T(8,128)(2,1)} %get-tuple-element.414, s32[]{:T(128)S(6)} %select_n.55, f32[2,512,1536]{2,1,0:T(8,128)} %get-tuple-element.374, ...), kind=kOutput, calls=%fused_computation.17.clone.1 | convolution fusion | flops 212535808 | bytes 26877960 | tf_op jit(solution)/shard_map/while/body/eval_jaxpr/hqk,qhd->khd/dot_general | solution.py:62
  502.5 14.9 %fusion.160 = bf16[3072,2,64]{0,2,1:T(8,128)(2,1)} fusion(bf16[3072,2,64]{0,2,1:T(8,128)(2,1)} %get-tuple-element.393, s32[]{:T(128)S(6)} %select_n.55, f32[2,512,1536]{2,1,0:T(8,128)} %fusion.159, bf16[3072,2,64]{0,2,1:T(8,128)(2,1)S(1)} %copy-done.6, s32[]{:T(128)S(6)} %min.12, f32[2,512,1536]{2,1,0:T(8,128)} %get-tuple-element.374, ...), kind=kOutput, calls=%fused_computation.27.clone.1 | convolution fusion | flops 212404736 | bytes 25698312 | tf_op jit(solution)/shard_map/while/body/eval_jaxpr/hqk,khd->qhd/dot_general | solution.py:59
  517.4 14.9 %fusion.161 = f32[1536,2,64]{0,2,1:T(8,128)S(1)} fusion(f32[2,512,1536]{2,1,0:T(8,128)} %fusion.159, f32[3072,2,64]{0,2,1:T(8,128)} %get-tuple-element.394, s32[]{:T(128)S(6)} %min.12, bf16[3072,2,64]{0,2,1:T(8,128)(2,1)} %get-tuple-element.414, s32[]{:T(128)S(6)} %select_n.55, f32[2,512,1536]{2,1,0:T(8,128)} %get-tuple-element.374, ...), kind=kOutput, calls=%fused_computation.17.clone.1 | convolution fusion | flops 212535808 | bytes 26877960 | tf_op jit(solution)/shard_map/while/body/eval_jaxpr/hqk,qhd->khd/dot_general | solution.py:62
  562.1 14.9 %fusion.160 = bf16[3072,2,64]{0,2,1:T(8,128)(2,1)} fusion(bf16[3072,2,64]{0,2,1:T(8,128)(2,1)} %get-tuple-element.393, s32[]{:T(128)S(6)} %select_n.55, f32[2,512,1536]{2,1,0:T(8,128)} %fusion.159, bf16[3072,2,64]{0,2,1:T(8,128)(2,1)S(1)} %copy-done.6, s32[]{:T(128)S(6)} %min.12, f32[2,512,1536]{2,1,0:T(8,128)} %get-tuple-element.374, ...), kind=kOutput, calls=%fused_computation.27.clone.1 | convolution fusion | flops 212404736 | bytes 25698312 | tf_op jit(solution)/shard_map/while/body/eval_jaxpr/hqk,khd->qhd/dot_general | solution.py:59
  577.0 15.0 %fusion.161 = f32[1536,2,64]{0,2,1:T(8,128)S(1)} fusion(f32[2,512,1536]{2,1,0:T(8,128)} %fusion.159, f32[3072,2,64]{0,2,1:T(8,128)} %get-tuple-element.394, s32[]{:T(128)S(6)} %min.12, bf16[3072,2,64]{0,2,1:T(8,128)(2,1)} %get-tuple-element.414, s32[]{:T(128)S(6)} %select_n.55, f32[2,512,1536]{2,1,0:T(8,128)} %get-tuple-element.374, ...), kind=kOutput, calls=%fused_computation.17.clone.1 | convolution fusion | flops 212535808 | bytes 26877960 | tf_op jit(solution)/shard_map/while/body/eval_jaxpr/hqk,qhd->khd/dot_general | solution.py:62
  615.6 40.9 %all_to_all.68 = bf16[3072,3,1,128]{3,1,2,0:T(4,128)(2,1)S(1)} all-to-all(bf16[3072,3,1,128]{3,1,2,0:T(4,128)(2,1)S(1)} %copy.83), channel_id=1, replica_groups=mesh['fsdp'=16,'seq'=8] {'seq'}, dimensions={0} | all-to-all | bytes 4718592 | tf_op jit(solution)/shard_map/all_to_all | solution.py:125
  659.4 9.5 %convolution_convert_fusion = bf16[1536,3072]{1,0:T(8,128)(2,1)} fusion(bf16[384,3072]{0,1:T(8,128)(2,1)} %bitcast.106, bf16[1,384,1536]{2,1,0:T(8,128)(2,1)S(1)} %copy-done.1, f32[384]{0:T(512)S(1)} %copy-done.10, f32[384]{0:T(512)S(1)} %copy-done.8), kind=kOutput, calls=%fused_computation.54 | convolution fusion | flops 3630956544 | bytes 12979200 | tf_op jit(solution)/shard_map/dot_general | solution.py:139
  671.8 15.6 %all_to_all.69 = bf16[8,2,24576]{2,1,0:T(2,128)(2,1)S(1)} all-to-all(bf16[8,2,24576]{2,1,0:T(2,128)(2,1)S(1)} %reshape.147), channel_id=1, replica_groups=mesh['fsdp'=16,'seq'=8] {'seq'}, dimensions={0} | all-to-all | bytes 1572864 | tf_op jit(solution)/shard_map/all_to_all | solution.py:124
  689.9 71.7 %reduce-scatter.5.cloned.1.call-done = bf16[96,3072]{1,0:T(8,128)(2,1)} async-done(((bf16[1536,3072]{1,0:T(8,128)(2,1)}), bf16[96,3072]{1,0:T(8,128)(2,1)}) %reduce-scatter.5.cloned.1.call-update) | async-done | bytes 589840 | tf_op jit(solution)/shard_map/reduce_scatter | solution.py:138
  763.8 7.7 fusion.108
  773.2 21.7 %reduce-scatter.7.cloned.1.call-done = bf16[384,96]{1,0:T(8,128)(2,1)} async-done(((bf16[3072,96]{1,0:T(8,128)(2,1)}), bf16[384,96]{1,0:T(8,128)(2,1)}) %reduce-scatter.7.cloned.1.call-update) | async-done | bytes 73744
  (134 shorter events, 231.8 us)
Async XLA Ops:
  13.1 8.4 %copy-start.5 = (bf16[1,384,1024]{2,1,0:T(8,128)(2,1)S(1)}, bf16[1,384,1024]{2,1,0:T(8,128)(2,1)}, u32[]{:S(2)}) copy-start(bf16[1,384,1024]{2,1,0:T(8,128)(2,1)} %param.9) | copy-start | bytes 2359300
  13.1 9.5 %copy-start = (bf16[1,384,1536]{2,1,0:T(8,128)(2,1)S(1)}, bf16[1,384,1536]{2,1,0:T(8,128)(2,1)}, u32[]{:S(2)}) copy-start(bf16[1,384,1536]{2,1,0:T(8,128)(2,1)} %param.6) | copy-start | bytes 3538948
  13.1 173.0 %all-to-all-start = ((bf16[16,96,3072]{2,1,0:T(8,128)(2,1)}), bf16[16,96,3072]{2,1,0:T(8,128)(2,1)}, u32[]{:S(2)}, u32[]{:S(2)}) async-start(bf16[16,96,3072]{2,1,0:T(8,128)(2,1)} %stack.10), calls=%async_computation | async-start | bytes 18874368 | tf_op jit(solution)/shard_map/all_to_all | solution.py:104
  22.8 175.5 %copy-start.7 = (f32[384]{0:T(512)}, f32[384]{0:T(512)S(1)}, u32[]{:S(2)}) copy-start(f32[384]{0:T(512)S(1)} %broadcast_multiply_fusion.2) | copy-start | bytes 4612
  23.3 175.0 %copy-start.9 = (f32[384]{0:T(512)}, f32[384]{0:T(512)S(1)}, u32[]{:S(2)}) copy-start(f32[384]{0:T(512)S(1)} %add_rsqrt_fusion) | copy-start | bytes 4612
  186.1 17.4 %all-to-all-start.2 = ((bf16[384,1,8,128]{0,3,1,2:T(8,128)(2,1)}), bf16[384,1,8,128]{0,3,1,2:T(8,128)(2,1)S(1)}, u32[]{:S(2)}, u32[]{:S(2)}) async-start(bf16[384,1,8,128]{0,3,1,2:T(8,128)(2,1)} %bitcast.17), calls=%async_computation.2 | async-start | bytes 1572864 | tf_op jit(solution)/shard_map/all_to_all | solution.py:111
  200.9 6.4 copy-start.11
  203.5 33.5 %all-to-all-start.1 = ((bf16[384,3,8,128]{3,0,1,2:T(8,128)(2,1)}), bf16[384,3,8,128]{3,0,1,2:T(8,128)(2,1)S(1)}, u32[]{:S(2)}, u32[]{:S(2)}) async-start(bf16[384,3,8,128]{3,0,1,2:T(8,128)(2,1)} %copy.74), calls=%async_computation.1 | async-start | bytes 4718592 | tf_op jit(solution)/shard_map/all_to_all | solution.py:110
  207.2 554.4 %reduce-scatter.5.cloned.1.call-start = ((), (), s32[]{:S(2)}) async-start(), calls=%async_computation.7 | async-start | bytes 10027008 | tf_op jit(solution)/shard_map/reduce_scatter | solution.py:138
  244.5 6.2 copy-start.6
  305.4 6.2 copy-start.6
  366.3 6.2 copy-start.6
  427.0 6.2 copy-start.6
  487.6 6.2 copy-start.6
  547.2 6.2 copy-start.6
  606.2 2.3 copy-start.3
  606.2 2.2 copy-start.2
  656.9 2.5 copy-start.1
  656.9 2.5 copy-start.8
  656.9 2.5 copy-start.10
  668.9 1.1 copy-start.4
  669.0 125.9 %reduce-scatter.7.cloned.1.call-start = ((), (), s32[]{:S(2)}) async-start(), calls=%async_computation.8 | async-start | bytes 884736
Sparse Core Ops, SparseCore 0:
  669.1 92.4 reduce-scatter.4
  764.0 30.8 reduce-scatter.6
